TPU v7x, 32 devices: a whole 2x2x4 slice. The times are simulated.
32 devices in a mesh: group: 2 (over y), frame: 4 (over z), row: 2 (over x), head: 2 (over core).
Axes of the slice: x: 2, y: 2, z: 4, core: 2. Of those that a mesh axis runs over, the one named last changes fastest.
Arguments:
- q_video: bfloat16 [16, 16, 16, 1536], P(('group', 'frame'), 'row', None, 'head'), parts along dimension 0, may hold values from -16 to 16
- k_video: bfloat16 [16, 16, 16, 1536], P(('group', 'frame'), 'row', None, 'head'), parts along dimension 0, may hold values from -8 to 8
- v_video: bfloat16 [16, 16, 16, 1536], P(('group', 'frame'), 'row', None, 'head'), parts along dimension 0, may hold values from -6 to 6
- q_reg: bfloat16 [256, 1536], P('group', 'head'), parts along dimension 0, may hold values from -16 to 16
- k_reg: bfloat16 [256, 1536], P('group', 'head'), parts along dimension 0, may hold values from -6 to 6
- v_reg: bfloat16 [256, 1536], P('group', 'head'), parts along dimension 0, may hold values from -6 to 6
- nbr_mask: int32 [4, 2, 2, 26], P('frame', 'row'), may hold values 0 or 1
Outputs:
- out_video: bfloat16 [16, 16, 16, 1536], P(('group', 'frame'), 'row', None, 'head'), parts along dimension 0
- out_reg: bfloat16 [256, 1536], P(('group', 'frame', 'row'), 'head'), parts along dimension 0
There are 2 independent parts, one for each index of `group`. A program takes and returns all parts, laid end to end along the dimension named above; an argument that names none is the same for every part. Nothing has to cross between parts.
All inputs are finite; a program needn't handle non-finite values. No bound on the sum of `nbr_mask` on one device may be relied on, other than what follows from the above.
Results may differ from a plain program's by a relative error of at most 0.0049.
Values may be sent and summed in bfloat16 or wider, within the bound.
A program may use at most 64 MiB of HBM per device.

v0:
```python
import jax
import jax.numpy as jnp
from jax import lax
from jax.sharding import PartitionSpec as P

HEAD_DIM = 128


def with_halo(array, sides, width):
    for axis, dim in sides:
        peers, length = (lax.axis_size(axis), array.shape[dim])
        up = [(i, (i + 1) % peers) for i in range(peers - 1)]
        down = [(j, i) for i, j in up]
        last = lax.slice_in_dim(array, length - width, length, axis=dim)
        first = lax.slice_in_dim(array, 0, width, axis=dim)
        before = lax.ppermute(last, axis, up)
        after = lax.ppermute(first, axis, down)
        array = jnp.concatenate([before, array, after], axis=dim)
    return array


def exact_product(weights, values):
    leading = weights.astype(values.dtype)
    remainder = (weights - leading.astype(weights.dtype)).astype(values.dtype)
    first = jnp.dot(leading, values, preferred_element_type=weights.dtype)
    return first + jnp.dot(remainder, values, preferred_element_type=weights.dtype)


def partial_softmax(query_rows, key_rows, value_rows, head_index, score_scale):
    query_head = lax.dynamic_slice_in_dim(query_rows, head_index * HEAD_DIM, HEAD_DIM, 1)
    key_head = lax.dynamic_slice_in_dim(key_rows, head_index * HEAD_DIM, HEAD_DIM, 1)
    value_head = lax.dynamic_slice_in_dim(value_rows, head_index * HEAD_DIM, HEAD_DIM, 1)
    scores = jnp.dot(query_head, key_head.T, preferred_element_type=jnp.float32) * score_scale
    row_max = jnp.max(scores, axis=-1)
    weights = jnp.exp(scores - row_max[:, None])
    weighted = exact_product(weights, value_head)
    return (row_max, jnp.sum(weights, axis=-1), weighted)


def per_head(query_rows, key_rows, value_rows, heads_dev, score_scale):

    def one_head(head_index):
        return partial_softmax(query_rows, key_rows, value_rows, head_index, score_scale)

    row_max, totals, weighted = lax.map(one_head, jnp.arange(heads_dev, dtype=jnp.int32))
    row_count = weighted.shape[1]
    return (
        row_max.T,
        totals.T,
        weighted.transpose(1, 0, 2).reshape(row_count, heads_dev * HEAD_DIM),
    )


def rescale(weighted, factor):
    row_count, heads_dev = factor.shape
    return (weighted.reshape(row_count, heads_dev, HEAD_DIM) * factor[:, :, None]).reshape(
        row_count, heads_dev * HEAD_DIM
    )


def combine(earlier, later):
    max_a, total_a, weighted_a = earlier
    max_b, total_b, weighted_b = later
    joint_max = jnp.maximum(max_a, max_b)
    factor_a = jnp.exp(max_a - joint_max)
    factor_b = jnp.exp(max_b - joint_max)
    return (
        joint_max,
        total_a * factor_a + total_b * factor_b,
        rescale(weighted_a, factor_a) + rescale(weighted_b, factor_b),
    )


def on_device(q_video, k_video, v_video, q_reg, k_reg, v_reg, nbr_mask):
    tile_f, tile_r, columns, features = q_video.shape
    col_tiles = nbr_mask.shape[2]
    tile_c = columns // col_tiles
    tile_size = tile_f * tile_r * tile_c
    heads_dev = features // HEAD_DIM
    registers = q_reg.shape[0]
    score_scale = HEAD_DIM ** (-0.5)
    frame_count = lax.axis_size("frame")
    rowdev_count = lax.axis_size("row")
    frame_pos = lax.axis_index("frame")
    rowdev_pos = lax.axis_index("row")
    paired = jnp.stack([k_video, v_video], 0)[None, None]
    near_block = with_halo(paired, (("frame", 0), ("row", 1)), 1)
    local_part = per_head(
        q_reg, k_video.reshape(-1, features), v_video.reshape(-1, features), heads_dev, score_scale
    )
    local_max, local_total, local_weighted = local_part
    row_share = registers // (frame_count * rowdev_count)
    row_start = (frame_pos * rowdev_count + rowdev_pos) * row_share
    own_queries = lax.dynamic_slice_in_dim(q_reg, row_start, row_share, 0)
    self_part = per_head(own_queries, k_reg, v_reg, heads_dev, score_scale)

    def own_rows(array):
        return lax.dynamic_slice_in_dim(array, row_start, row_share, 0)

    global_max = lax.pmax(local_max, ("frame", "row"))
    factor = jnp.exp(local_max - global_max)
    reduced = lax.psum((rescale(local_weighted, factor), local_total * factor), ("frame", "row"))
    collected = (own_rows(global_max), own_rows(reduced[1]), own_rows(reduced[0]))
    final_max, final_total, final_weighted = combine(collected, self_part)
    out_reg = (
        (final_weighted.reshape(row_share, heads_dev, HEAD_DIM) / final_total[:, :, None])
        .reshape(row_share, features)
        .astype(jnp.bfloat16)
    )
    near_block = near_block.reshape(3, 3, 2, tile_f, tile_r, col_tiles, tile_c, features)
    queries = (
        q_video.reshape(tile_f, tile_r, col_tiles, tile_c, features)
        .transpose(2, 0, 1, 3, 4)
        .reshape(col_tiles, tile_size, features)
    )
    window = min(3, col_tiles)
    full_mask = jnp.concatenate(
        [nbr_mask[0, 0, :, :13], jnp.ones((col_tiles, 1), jnp.int32), nbr_mask[0, 0, :, 13:]], 1
    )
    offsets = jnp.arange(3, dtype=jnp.int32) - 1
    frame_inside = (frame_pos + offsets >= 0) & (frame_pos + offsets < frame_count)
    row_inside = (rowdev_pos + offsets >= 0) & (rowdev_pos + offsets < rowdev_count)

    def one_item(item_index):
        col_index = item_index // heads_dev
        head_index = item_index % heads_dev
        first_col = jnp.clip(col_index - 1, 0, col_tiles - window)
        anchor = jnp.zeros((), jnp.int32)
        near_piece = lax.dynamic_slice(
            near_block,
            (anchor, anchor, anchor, anchor, anchor, first_col, anchor, head_index * HEAD_DIM),
            (3, 3, 2, tile_f, tile_r, window, tile_c, HEAD_DIM),
        )
        near_head = near_piece.transpose(2, 0, 1, 5, 3, 4, 6, 7).reshape(
            2, 3, 3, window, tile_size, HEAD_DIM
        )
        key_cols = first_col + jnp.arange(window, dtype=jnp.int32)
        offset_codes = (
            (offsets[:, None, None] + 1) * 9
            + (offsets[None, :, None] + 1) * 3
            + (key_cols - col_index + 1)[None, None, :]
        )
        mask_row = lax.dynamic_index_in_dim(full_mask, col_index, 0, keepdims=False)
        picked = jnp.sum(
            jnp.where(offset_codes[..., None] == jnp.arange(27, dtype=jnp.int32), mask_row, 0),
            axis=-1,
        )
        adjacent = jnp.abs(key_cols - col_index) <= 1
        allowed = (
            (picked == 1)
            & frame_inside[:, None, None]
            & row_inside[None, :, None]
            & adjacent[None, None, :]
        )
        key_ok = jnp.concatenate(
            [
                jnp.repeat(
                    allowed.reshape(-1), tile_size, total_repeat_length=9 * window * tile_size
                ),
                jnp.ones((registers,), bool),
            ]
        )
        key_rows = jnp.concatenate(
            [
                near_head[0].reshape(-1, HEAD_DIM),
                lax.dynamic_slice_in_dim(k_reg, head_index * HEAD_DIM, HEAD_DIM, 1),
            ],
            0,
        )
        value_rows = jnp.concatenate(
            [
                near_head[1].reshape(-1, HEAD_DIM),
                lax.dynamic_slice_in_dim(v_reg, head_index * HEAD_DIM, HEAD_DIM, 1),
            ],
            0,
        )
        query_head = lax.dynamic_slice(
            queries, (col_index, anchor, head_index * HEAD_DIM), (1, tile_size, HEAD_DIM)
        )[0]
        scores = jnp.dot(query_head, key_rows.T, preferred_element_type=jnp.float32) * score_scale
        scores = jnp.where(key_ok[None, :], scores, -jnp.inf)
        weights = jax.nn.softmax(scores, axis=-1).astype(jnp.bfloat16)
        return jnp.dot(weights, value_rows, preferred_element_type=jnp.float32).astype(jnp.bfloat16)

    results = lax.map(one_item, jnp.arange(col_tiles * heads_dev, dtype=jnp.int32))
    out_video = (
        results.reshape(col_tiles, heads_dev, tile_f, tile_r, tile_c, HEAD_DIM)
        .transpose(2, 3, 0, 4, 1, 5)
        .reshape(tile_f, tile_r, columns, features)
    )
    return (out_video, out_reg)


def solution(mesh):
    return jax.shard_map(
        on_device,
        mesh=mesh,
        in_specs=(
            P(("group", "frame"), "row", None, "head"),
            P(("group", "frame"), "row", None, "head"),
            P(("group", "frame"), "row", None, "head"),
            P("group", "head"),
            P("group", "head"),
            P("group", "head"),
            P("frame", "row", None, None),
        ),
        out_specs=(
            P(("group", "frame"), "row", None, "head"),
            P(("group", "frame", "row"), "head"),
        ),
        check_vma=False,
    )
```

profile of v0, /device:TPU:0, one launch (start us, length us, event | category | flops | bytes accessed | tf_op | source)
XLA Modules:
  0.0 386.3 jit_solution(3703701731983514804)
XLA Ops:
  8.4 5.0 %collective-permute-start = (bf16[1,1,2,2,8,16,768]{6,5,4,3,2,1,0:T(8,128)(2,1)S(1)}, bf16[1,1,2,2,8,16,768]{6,5,4,3,2,1,0:T(8,128)(2,1)S(1)}, u32[]{:S(2)}, u32[]{:S(2)}) collective-permute-start(bf16[1,1,2,2,8,16,768]{6,5,4,3,2,1,0:T(8,128)(2,1)S(1)} %maximum_bitcast_fusion.1), channel_id=1, source_target_pairs={{0,4},{4,8},{8,12},{1,5},{5,9},{9,13},{2,6},{6,10},{10,14},{3,7},{... | collective-permute-start | bytes 2359304 | tf_op jit(solution)/shard_map/ppermute | solution.py:16
  13.4 1.3 collective-permute-start.1
  14.7 29.3 %while.46 = (s32[]{:T(128)}, f32[6,128]{1,0:T(8,128)S(1)}, f32[6,128]{1,0:T(8,128)S(1)}, f32[6,128,128]{1,2,0:T(8,128)S(1)}, s32[6]{0:T(128)S(1)}, /*index=5*/bf...) while((s32[]{:T(128)}, f32[6,128]{1,0:T(8,128)S(1)}, ...), condition=%wide.region_8.9_spmd, body=%wide.region_5.0_spmd.sunk | while | flops 25542404 | bytes 1218243 | solution.py:45
  44.0 22.7 %pmax.7 = f32[128,6]{0,1:T(8,128)S(1)} all-reduce(f32[128,6]{0,1:T(8,128)S(1)} %bitcast.239), channel_id=1, replica_groups=mesh['group'=2,'frame'=4,'row'=2,'head'=2] {'frame','row'}, use_global_device_ids=true, to_apply=%region_9.10 | all-reduce | flops 768 | bytes 6144 | tf_op jit(solution)/shard_map/pmax | solution.py:100
  68.6 1.7 pad_maximum_fusion
  70.2 2.8 collective-permute-start.2
  73.1 1.3 collective-permute-start.3
  74.4 17.6 %while.47 = (s32[]{:T(128)}, f32[6,16]{1,0:T(8,128)S(1)}, f32[6,16]{1,0:T(8,128)S(1)}, f32[6,16,128]{2,1,0:T(8,128)S(1)}, s32[6]{0:T(128)S(1)}, /*index=5*/bf16[...) while((s32[]{:T(128)}, f32[6,16]{1,0:T(8,128)S(1)}, ...), condition=%wide.region_14.15_spmd, body=%wide.region_11.14_spmd.sunk | while | flops 1597414 | bytes 162435 | solution.py:45
  92.0 43.7 %psum.15 = f32[128,6]{0,1:T(8,128)S(1)} all-reduce(f32[128,6]{0,1:T(8,128)S(1)} %get-tuple-element.582), channel_id=1, replica_groups=mesh['group'=2,'frame'=4,'row'=2,'head'=2] {'frame','row'}, use_global_device_ids=true, to_apply=%region_15.16 | all-reduce | flops 768 | bytes 6144 | tf_op jit(solution)/shard_map/psum | solution.py:102
  137.6 1.5 fusion.61
  139.1 5.9 %maximum_bitcast_fusion = bf16[3,3,2,2,8,2,8,768]{7,6,5,4,3,2,1,0:T(8,128)(2,1)} fusion(bf16[3,1,2,2,8,16,768]{6,5,4,3,2,1,0:T(8,128)(2,1)} %collective-permute-done.3, bf16[1,1,2,2,8,16,768]{6,5,4,3,2,1,0:T(8,128)(2,1)S(1)} %collective-permute-done.1, bf16[1,1,2,2,8,16,768]{6,5,4,3,2,1,0:T(8,128)(2,1)S(1)} %maximum_bitcast_fusion.1, ...), kind=kLoop, calls=%fused_computation.100 | loop fusion | flops 14155776 | bytes 14155776 | tf_op jit(solution)/shard_map/reshape | solution.py:110
  145.0 233.7 %while.48 = (s32[]{:T(128)}, bf16[12,128,128]{2,1,0:T(8,128)(2,1)S(1)}, s32[12]{0:T(128)S(1)}, s32[2,27]{1,0:T(2,128)S(1)}, bf16[2,128,768]{2,1,0:T(8,128)(2,1)S...) while((s32[]{:T(128)}, ...), condition=%wide.region_4.5_spmd.clone, body=%wide.region_0.4_spmd.clone.sunk | while | flops 164492608 | bytes 10002113 | solution.py:185
  149.0 4.7 %select_reduce_fusion.2 = (pred[2304]{0:T(1024)(128)(4,1)S(1)}, pred[2304]{0:T(1024)(128)(4,1)S(1)}, pred[2304]{0:T(1024)(128)(4,1)S(1)}, pred[2304]{0:T(1024)(1...) fusion(pred[]{:T(512)} %bitcast.204, ...), kind=kLoop, calls=%fused_computation.55.clone.1 | loop fusion | flops 57600 | bytes 46087 | tf_op jit(solution)/shard_map/while/body/eval_jaxpr/jit(_take)/gather | solution.py:157
  153.7 7.0 %fusion.121 = pred[2304]{0:T(1024)(128)(4,1)S(1)} fusion(pred[2304]{0:T(1024)(128)(4,1)S(1)} %get-tuple-element.846, pred[2304]{0:T(1024)(128)(4,1)S(1)} %get-tuple-element.847, pred[2304]{0:T(1024)(128)(4,1)S(1)} %get-tuple-element.848, pred[2304]{0:T(1024)(128)(4,1)S(1)} %get-tuple-element.849, pred[2304]{0:T(1024)(128)(4,1)S(1)} %get-tuple-element.850, ...), kind=kLoop, calls=%fused_computation.79.clone.1 | loop fusion | flops 46080 | bytes 29963 | tf_op jit(solution)/shard_map/while/body/eval_jaxpr/jit(_take)/select_n | solution.py:157
  161.5 1.6 copy_bitcast_fusion.3
  168.5 4.7 %select_reduce_fusion.2 = (pred[2304]{0:T(1024)(128)(4,1)S(1)}, pred[2304]{0:T(1024)(128)(4,1)S(1)}, pred[2304]{0:T(1024)(128)(4,1)S(1)}, pred[2304]{0:T(1024)(1...) fusion(pred[]{:T(512)} %bitcast.204, ...), kind=kLoop, calls=%fused_computation.55.clone.1 | loop fusion | flops 57600 | bytes 46087 | tf_op jit(solution)/shard_map/while/body/eval_jaxpr/jit(_take)/gather | solution.py:157
  173.2 7.0 %fusion.121 = pred[2304]{0:T(1024)(128)(4,1)S(1)} fusion(pred[2304]{0:T(1024)(128)(4,1)S(1)} %get-tuple-element.846, pred[2304]{0:T(1024)(128)(4,1)S(1)} %get-tuple-element.847, pred[2304]{0:T(1024)(128)(4,1)S(1)} %get-tuple-element.848, pred[2304]{0:T(1024)(128)(4,1)S(1)} %get-tuple-element.849, pred[2304]{0:T(1024)(128)(4,1)S(1)} %get-tuple-element.850, ...), kind=kLoop, calls=%fused_computation.79.clone.1 | loop fusion | flops 46080 | bytes 29963 | tf_op jit(solution)/shard_map/while/body/eval_jaxpr/jit(_take)/select_n | solution.py:157
  181.0 1.6 copy_bitcast_fusion.3
  187.9 4.7 %select_reduce_fusion.2 = (pred[2304]{0:T(1024)(128)(4,1)S(1)}, pred[2304]{0:T(1024)(128)(4,1)S(1)}, pred[2304]{0:T(1024)(128)(4,1)S(1)}, pred[2304]{0:T(1024)(1...) fusion(pred[]{:T(512)} %bitcast.204, ...), kind=kLoop, calls=%fused_computation.55.clone.1 | loop fusion | flops 57600 | bytes 46087 | tf_op jit(solution)/shard_map/while/body/eval_jaxpr/jit(_take)/gather | solution.py:157
  192.6 7.0 %fusion.121 = pred[2304]{0:T(1024)(128)(4,1)S(1)} fusion(pred[2304]{0:T(1024)(128)(4,1)S(1)} %get-tuple-element.846, pred[2304]{0:T(1024)(128)(4,1)S(1)} %get-tuple-element.847, pred[2304]{0:T(1024)(128)(4,1)S(1)} %get-tuple-element.848, pred[2304]{0:T(1024)(128)(4,1)S(1)} %get-tuple-element.849, pred[2304]{0:T(1024)(128)(4,1)S(1)} %get-tuple-element.850, ...), kind=kLoop, calls=%fused_computation.79.clone.1 | loop fusion | flops 46080 | bytes 29963 | tf_op jit(solution)/shard_map/while/body/eval_jaxpr/jit(_take)/select_n | solution.py:157
  200.4 1.6 copy_bitcast_fusion.3
  207.4 4.7 %select_reduce_fusion.2 = (pred[2304]{0:T(1024)(128)(4,1)S(1)}, pred[2304]{0:T(1024)(128)(4,1)S(1)}, pred[2304]{0:T(1024)(128)(4,1)S(1)}, pred[2304]{0:T(1024)(1...) fusion(pred[]{:T(512)} %bitcast.204, ...), kind=kLoop, calls=%fused_computation.55.clone.1 | loop fusion | flops 57600 | bytes 46087 | tf_op jit(solution)/shard_map/while/body/eval_jaxpr/jit(_take)/gather | solution.py:157
  212.1 7.0 %fusion.121 = pred[2304]{0:T(1024)(128)(4,1)S(1)} fusion(pred[2304]{0:T(1024)(128)(4,1)S(1)} %get-tuple-element.846, pred[2304]{0:T(1024)(128)(4,1)S(1)} %get-tuple-element.847, pred[2304]{0:T(1024)(128)(4,1)S(1)} %get-tuple-element.848, pred[2304]{0:T(1024)(128)(4,1)S(1)} %get-tuple-element.849, pred[2304]{0:T(1024)(128)(4,1)S(1)} %get-tuple-element.850, ...), kind=kLoop, calls=%fused_computation.79.clone.1 | loop fusion | flops 46080 | bytes 29963 | tf_op jit(solution)/shard_map/while/body/eval_jaxpr/jit(_take)/select_n | solution.py:157
  219.9 1.6 copy_bitcast_fusion.3
  226.9 4.7 %select_reduce_fusion.2 = (pred[2304]{0:T(1024)(128)(4,1)S(1)}, pred[2304]{0:T(1024)(128)(4,1)S(1)}, pred[2304]{0:T(1024)(128)(4,1)S(1)}, pred[2304]{0:T(1024)(1...) fusion(pred[]{:T(512)} %bitcast.204, ...), kind=kLoop, calls=%fused_computation.55.clone.1 | loop fusion | flops 57600 | bytes 46087 | tf_op jit(solution)/shard_map/while/body/eval_jaxpr/jit(_take)/gather | solution.py:157
  231.6 7.0 %fusion.121 = pred[2304]{0:T(1024)(128)(4,1)S(1)} fusion(pred[2304]{0:T(1024)(128)(4,1)S(1)} %get-tuple-element.846, pred[2304]{0:T(1024)(128)(4,1)S(1)} %get-tuple-element.847, pred[2304]{0:T(1024)(128)(4,1)S(1)} %get-tuple-element.848, pred[2304]{0:T(1024)(128)(4,1)S(1)} %get-tuple-element.849, pred[2304]{0:T(1024)(128)(4,1)S(1)} %get-tuple-element.850, ...), kind=kLoop, calls=%fused_computation.79.clone.1 | loop fusion | flops 46080 | bytes 29963 | tf_op jit(solution)/shard_map/while/body/eval_jaxpr/jit(_take)/select_n | solution.py:157
  239.4 1.6 copy_bitcast_fusion.3
  246.4 4.7 %select_reduce_fusion.2 = (pred[2304]{0:T(1024)(128)(4,1)S(1)}, pred[2304]{0:T(1024)(128)(4,1)S(1)}, pred[2304]{0:T(1024)(128)(4,1)S(1)}, pred[2304]{0:T(1024)(1...) fusion(pred[]{:T(512)} %bitcast.204, ...), kind=kLoop, calls=%fused_computation.55.clone.1 | loop fusion | flops 57600 | bytes 46087 | tf_op jit(solution)/shard_map/while/body/eval_jaxpr/jit(_take)/gather | solution.py:157
  251.1 7.0 %fusion.121 = pred[2304]{0:T(1024)(128)(4,1)S(1)} fusion(pred[2304]{0:T(1024)(128)(4,1)S(1)} %get-tuple-element.846, pred[2304]{0:T(1024)(128)(4,1)S(1)} %get-tuple-element.847, pred[2304]{0:T(1024)(128)(4,1)S(1)} %get-tuple-element.848, pred[2304]{0:T(1024)(128)(4,1)S(1)} %get-tuple-element.849, pred[2304]{0:T(1024)(128)(4,1)S(1)} %get-tuple-element.850, ...), kind=kLoop, calls=%fused_computation.79.clone.1 | loop fusion | flops 46080 | bytes 29963 | tf_op jit(solution)/shard_map/while/body/eval_jaxpr/jit(_take)/select_n | solution.py:157
  258.9 1.6 copy_bitcast_fusion.3
  265.8 4.7 %select_reduce_fusion.2 = (pred[2304]{0:T(1024)(128)(4,1)S(1)}, pred[2304]{0:T(1024)(128)(4,1)S(1)}, pred[2304]{0:T(1024)(128)(4,1)S(1)}, pred[2304]{0:T(1024)(1...) fusion(pred[]{:T(512)} %bitcast.204, ...), kind=kLoop, calls=%fused_computation.55.clone.1 | loop fusion | flops 57600 | bytes 46087 | tf_op jit(solution)/shard_map/while/body/eval_jaxpr/jit(_take)/gather | solution.py:157
  270.5 7.0 %fusion.121 = pred[2304]{0:T(1024)(128)(4,1)S(1)} fusion(pred[2304]{0:T(1024)(128)(4,1)S(1)} %get-tuple-element.846, pred[2304]{0:T(1024)(128)(4,1)S(1)} %get-tuple-element.847, pred[2304]{0:T(1024)(128)(4,1)S(1)} %get-tuple-element.848, pred[2304]{0:T(1024)(128)(4,1)S(1)} %get-tuple-element.849, pred[2304]{0:T(1024)(128)(4,1)S(1)} %get-tuple-element.850, ...), kind=kLoop, calls=%fused_computation.79.clone.1 | loop fusion | flops 46080 | bytes 29963 | tf_op jit(solution)/shard_map/while/body/eval_jaxpr/jit(_take)/select_n | solution.py:157
  278.4 1.6 copy_bitcast_fusion.3
  285.3 4.7 %select_reduce_fusion.2 = (pred[2304]{0:T(1024)(128)(4,1)S(1)}, pred[2304]{0:T(1024)(128)(4,1)S(1)}, pred[2304]{0:T(1024)(128)(4,1)S(1)}, pred[2304]{0:T(1024)(1...) fusion(pred[]{:T(512)} %bitcast.204, ...), kind=kLoop, calls=%fused_computation.55.clone.1 | loop fusion | flops 57600 | bytes 46087 | tf_op jit(solution)/shard_map/while/body/eval_jaxpr/jit(_take)/gather | solution.py:157
  290.0 7.0 %fusion.121 = pred[2304]{0:T(1024)(128)(4,1)S(1)} fusion(pred[2304]{0:T(1024)(128)(4,1)S(1)} %get-tuple-element.846, pred[2304]{0:T(1024)(128)(4,1)S(1)} %get-tuple-element.847, pred[2304]{0:T(1024)(128)(4,1)S(1)} %get-tuple-element.848, pred[2304]{0:T(1024)(128)(4,1)S(1)} %get-tuple-element.849, pred[2304]{0:T(1024)(128)(4,1)S(1)} %get-tuple-element.850, ...), kind=kLoop, calls=%fused_computation.79.clone.1 | loop fusion | flops 46080 | bytes 29963 | tf_op jit(solution)/shard_map/while/body/eval_jaxpr/jit(_take)/select_n | solution.py:157
  297.8 1.6 copy_bitcast_fusion.3
  304.8 4.7 %select_reduce_fusion.2 = (pred[2304]{0:T(1024)(128)(4,1)S(1)}, pred[2304]{0:T(1024)(128)(4,1)S(1)}, pred[2304]{0:T(1024)(128)(4,1)S(1)}, pred[2304]{0:T(1024)(1...) fusion(pred[]{:T(512)} %bitcast.204, ...), kind=kLoop, calls=%fused_computation.55.clone.1 | loop fusion | flops 57600 | bytes 46087 | tf_op jit(solution)/shard_map/while/body/eval_jaxpr/jit(_take)/gather | solution.py:157
  309.5 7.0 %fusion.121 = pred[2304]{0:T(1024)(128)(4,1)S(1)} fusion(pred[2304]{0:T(1024)(128)(4,1)S(1)} %get-tuple-element.846, pred[2304]{0:T(1024)(128)(4,1)S(1)} %get-tuple-element.847, pred[2304]{0:T(1024)(128)(4,1)S(1)} %get-tuple-element.848, pred[2304]{0:T(1024)(128)(4,1)S(1)} %get-tuple-element.849, pred[2304]{0:T(1024)(128)(4,1)S(1)} %get-tuple-element.850, ...), kind=kLoop, calls=%fused_computation.79.clone.1 | loop fusion | flops 46080 | bytes 29963 | tf_op jit(solution)/shard_map/while/body/eval_jaxpr/jit(_take)/select_n | solution.py:157
  317.3 1.6 copy_bitcast_fusion.3
  324.3 4.7 %select_reduce_fusion.2 = (pred[2304]{0:T(1024)(128)(4,1)S(1)}, pred[2304]{0:T(1024)(128)(4,1)S(1)}, pred[2304]{0:T(1024)(128)(4,1)S(1)}, pred[2304]{0:T(1024)(1...) fusion(pred[]{:T(512)} %bitcast.204, ...), kind=kLoop, calls=%fused_computation.55.clone.1 | loop fusion | flops 57600 | bytes 46087 | tf_op jit(solution)/shard_map/while/body/eval_jaxpr/jit(_take)/gather | solution.py:157
  329.0 7.0 %fusion.121 = pred[2304]{0:T(1024)(128)(4,1)S(1)} fusion(pred[2304]{0:T(1024)(128)(4,1)S(1)} %get-tuple-element.846, pred[2304]{0:T(1024)(128)(4,1)S(1)} %get-tuple-element.847, pred[2304]{0:T(1024)(128)(4,1)S(1)} %get-tuple-element.848, pred[2304]{0:T(1024)(128)(4,1)S(1)} %get-tuple-element.849, pred[2304]{0:T(1024)(128)(4,1)S(1)} %get-tuple-element.850, ...), kind=kLoop, calls=%fused_computation.79.clone.1 | loop fusion | flops 46080 | bytes 29963 | tf_op jit(solution)/shard_map/while/body/eval_jaxpr/jit(_take)/select_n | solution.py:157
  336.8 1.6 copy_bitcast_fusion.3
  343.7 4.7 %select_reduce_fusion.2 = (pred[2304]{0:T(1024)(128)(4,1)S(1)}, pred[2304]{0:T(1024)(128)(4,1)S(1)}, pred[2304]{0:T(1024)(128)(4,1)S(1)}, pred[2304]{0:T(1024)(1...) fusion(pred[]{:T(512)} %bitcast.204, ...), kind=kLoop, calls=%fused_computation.55.clone.1 | loop fusion | flops 57600 | bytes 46087 | tf_op jit(solution)/shard_map/while/body/eval_jaxpr/jit(_take)/gather | solution.py:157
  348.4 7.0 %fusion.121 = pred[2304]{0:T(1024)(128)(4,1)S(1)} fusion(pred[2304]{0:T(1024)(128)(4,1)S(1)} %get-tuple-element.846, pred[2304]{0:T(1024)(128)(4,1)S(1)} %get-tuple-element.847, pred[2304]{0:T(1024)(128)(4,1)S(1)} %get-tuple-element.848, pred[2304]{0:T(1024)(128)(4,1)S(1)} %get-tuple-element.849, pred[2304]{0:T(1024)(128)(4,1)S(1)} %get-tuple-element.850, ...), kind=kLoop, calls=%fused_computation.79.clone.1 | loop fusion | flops 46080 | bytes 29963 | tf_op jit(solution)/shard_map/while/body/eval_jaxpr/jit(_take)/select_n | solution.py:157
  356.3 1.6 copy_bitcast_fusion.3
  363.2 4.7 %select_reduce_fusion.2 = (pred[2304]{0:T(1024)(128)(4,1)S(1)}, pred[2304]{0:T(1024)(128)(4,1)S(1)}, pred[2304]{0:T(1024)(128)(4,1)S(1)}, pred[2304]{0:T(1024)(1...) fusion(pred[]{:T(512)} %bitcast.204, ...), kind=kLoop, calls=%fused_computation.55.clone.1 | loop fusion | flops 57600 | bytes 46087 | tf_op jit(solution)/shard_map/while/body/eval_jaxpr/jit(_take)/gather | solution.py:157
  367.9 7.0 %fusion.121 = pred[2304]{0:T(1024)(128)(4,1)S(1)} fusion(pred[2304]{0:T(1024)(128)(4,1)S(1)} %get-tuple-element.846, pred[2304]{0:T(1024)(128)(4,1)S(1)} %get-tuple-element.847, pred[2304]{0:T(1024)(128)(4,1)S(1)} %get-tuple-element.848, pred[2304]{0:T(1024)(128)(4,1)S(1)} %get-tuple-element.849, pred[2304]{0:T(1024)(128)(4,1)S(1)} %get-tuple-element.850, ...), kind=kLoop, calls=%fused_computation.79.clone.1 | loop fusion | flops 46080 | bytes 29963 | tf_op jit(solution)/shard_map/while/body/eval_jaxpr/jit(_take)/select_n | solution.py:157
  375.7 1.6 copy_bitcast_fusion.3
  (364 shorter events, 93.6 us)
Async XLA Ops:
  7.2 130.2 %all-reduce.3.cloned.1.call-start = ((), (), s32[]{:S(2)}) async-start(), calls=%async_computation | async-start | bytes 786432 | tf_op jit(solution)/shard_map/psum | solution.py:102
  8.4 60.2 %collective-permute-start = (bf16[1,1,2,2,8,16,768]{6,5,4,3,2,1,0:T(8,128)(2,1)S(1)}, bf16[1,1,2,2,8,16,768]{6,5,4,3,2,1,0:T(8,128)(2,1)S(1)}, u32[]{:S(2)}, u32[]{:S(2)}) collective-permute-start(bf16[1,1,2,2,8,16,768]{6,5,4,3,2,1,0:T(8,128)(2,1)S(1)} %maximum_bitcast_fusion.1), channel_id=1, source_target_pairs={{0,4},{4,8},{8,12},{1,5},{5,9},{9,13},{2,6},{6,10},{10,14},{3,7},{... | collective-permute-start | bytes 2359304 | tf_op jit(solution)/shard_map/ppermute | solution.py:16
  13.4 55.2 %collective-permute-start.1 = (bf16[1,1,2,2,8,16,768]{6,5,4,3,2,1,0:T(8,128)(2,1)S(1)}, bf16[1,1,2,2,8,16,768]{6,5,4,3,2,1,0:T(8,128)(2,1)S(1)}, u32[]{:S(2)}, u32[]{:S(2)}) collective-permute-start(bf16[1,1,2,2,8,16,768]{6,5,4,3,2,1,0:T(8,128)(2,1)S(1)} %maximum_bitcast_fusion.1), channel_id=1, source_target_pairs={{4,0},{8,4},{12,8},{5,1},{9,5},{13,9},{6,2},{10,6},{14,10},{7,3},{... | collective-permute-start | bytes 2359304 | tf_op jit(solution)/shard_map/ppermute | solution.py:17
  68.5 5.8 %copy-start.2 = (bf16[128,768]{1,0:T(8,128)(2,1)S(1)}, bf16[128,768]{1,0:T(8,128)(2,1)}, u32[]{:S(2)}) copy-start(bf16[128,768]{1,0:T(8,128)(2,1)} %param.20) | copy-start | bytes 589828
  68.6 67.5 %copy-start = (bf16[2,8,16,768]{3,2,1,0:T(8,128)(2,1)S(1)}, bf16[2,8,16,768]{3,2,1,0:T(8,128)(2,1)}, u32[]{:S(2)}) copy-start(bf16[2,8,16,768]{3,2,1,0:T(8,128)(2,1)} %param.15) | copy-start | bytes 1179652
  70.2 65.8 %copy-start.3 = (s32[1,1,2,26]{3,2,1,0:T(2,128)S(1)}, s32[1,1,2,26]{3,2,1,0:T(2,128)}, u32[]{:S(2)}) copy-start(s32[1,1,2,26]{3,2,1,0:T(2,128)} %param.21) | copy-start | bytes 628
  70.2 68.8 %collective-permute-start.2 = (bf16[3,1,2,2,8,16,768]{6,5,4,3,2,1,0:T(8,128)(2,1)}, bf16[3,1,2,2,8,16,768]{6,5,4,3,2,1,0:T(8,128)(2,1)}, u32[]{:S(2)}, u32[]{:S(2)}) collective-permute-start(bf16[3,1,2,2,8,16,768]{6,5,4,3,2,1,0:T(8,128)(2,1)} %pad_maximum_fusion), channel_id=1, source_target_pairs={{0,2},{1,3},{4,6},{5,7},{8,10},{9,11},{12,14},{13,15},{16,18},{17,... | collective-permute-start | bytes 7077896 | tf_op jit(solution)/shard_map/ppermute | solution.py:16
  73.1 66.0 %collective-permute-start.3 = (bf16[3,1,2,2,8,16,768]{6,5,4,3,2,1,0:T(8,128)(2,1)}, bf16[3,1,2,2,8,16,768]{6,5,4,3,2,1,0:T(8,128)(2,1)}, u32[]{:S(2)}, u32[]{:S(2)}) collective-permute-start(bf16[3,1,2,2,8,16,768]{6,5,4,3,2,1,0:T(8,128)(2,1)} %pad_maximum_fusion), channel_id=1, source_target_pairs={{2,0},{3,1},{6,4},{7,5},{10,8},{11,9},{14,12},{15,13},{18,16},{19,... | collective-permute-start | bytes 7077896 | tf_op jit(solution)/shard_map/ppermute | solution.py:17
  139.1 5.9 %copy-start.1 = (bf16[12,128,128]{2,1,0:T(8,128)(2,1)S(1)}, bf16[12,128,128]{2,1,0:T(8,128)(2,1)}, u32[]{:S(2)}) copy-start(bf16[12,128,128]{2,1,0:T(8,128)(2,1)} %custom-call.6) | copy-start | bytes 1179652
Sparse Core Ops, SparseCore 0:
  67.9 69.4 all-reduce.2
where the time goes:
time: 392 us; the launch traced here: 386 us
  other arithmetic  164 us (42%)
  blocking collectives  66.4 us (17%)
  local copies, waits for them, and re-layouts  58.4 us (15%)
  matrix products  38.3 us (10%)
  loops' own time  33.3 us (8%)
  between operations  14.2 us (4%)
  starting transfers between devices  10.4 us (3%)
    select_n x12, other arithmetic, one_item(): jnp.repeat(allowed.reshape(-1), tile_size, total_repeat_length=9 * window...  84.1 us
    gather x12, other arithmetic, one_item(): jnp.repeat(allowed.reshape(-1), tile_size, total_repeat_length=9 * window...  56.4 us
    psum x1, blocking collectives, on_device(): lax.psum((rescale(local_weighted, factor), local_total * factor), ('frame...  43.7 us
    another operation x1, loops' own time, on_device(): lax.map(one_item, jnp.arange(col_tiles * heads_dev, dtype=jnp.int32))  25 us
    pmax x1, blocking collectives, on_device(): global_max = lax.pmax(local_max, ('frame', 'row'))  22.7 us
    transpose x12, local copies, waits for them, and re-layouts, one_item(): near_piece.transpose(2, 0, 1, 5, 3, 4, 6, 7)  18.9 us
    dot_general x12, matrix products, partial_softmax(): jnp.dot(query_head, key_head.T, preferred_element_type=jnp.float32)  12.8 us
    dynamic_slice x12, local copies, waits for them, and re-layouts, one_item(): lax.dynamic_slice_in_dim(v_reg, head_index * HEAD_DIM, HEAD_DIM, 1)  9.27 us
  transfers between devices with their start and end apart: 5, of which 1 were waited for; matrix products, arithmetic and copies ran while one was open for 11% of the time, Pallas kernels for 0%

commit v1 on v0

v1 whole, which is shorter than its diff:
```python
import functools

import jax
import jax.numpy as jnp
from jax import lax
from jax.experimental import pallas as pl
from jax.experimental.pallas import tpu as pltpu
from jax.sharding import PartitionSpec as P

HEAD_DIM = 128
NEG = -1e30
SCALE = HEAD_DIM ** -0.5
LOG2E = 1.4426950408889634
MESH = pl.DeviceIdType.MESH
SLOT_DF = (0, -1, 1)


def offset_index(df, dr, dc):
    code = 9 * (df + 1) + 3 * (dr + 1) + (dc + 1)
    return code - 1 if code > 13 else code


def nt(a, b):
    return lax.dot_general(a, b, (((1,), (1,)), ((), ())), preferred_element_type=jnp.float32)


def tn(a, b):
    return lax.dot_general(a, b, (((0,), (0,)), ((), ())), preferred_element_type=jnp.float32)


def block_kernel(dims, *refs):
    (heads, tokens, columns, tile_c, col_tiles, regs, n_frame, n_row, with_regs) = dims
    peers = n_frame * n_row
    share = regs // peers
    nbrs = 0 if n_row == 1 else (1 if n_row == 2 else 2)
    if with_regs:
        (q_hbm, k_hbm, v_hbm, qr_ref, kr_ref, vr_ref, mask_ref, out_ref, outr_ref,
         qbuf, kv, bias, bias_out, s_ref, o_own, st_own, o_out, st_out, o_in, st_in,
         ld_sem, zs, zr, xs, xr, bs, br, osd, orv, sts, str_,
         r_out, rst_t, rst_out, r_in, rst_in, rs, rr) = refs
    else:
        (q_hbm, k_hbm, v_hbm, kr_ref, vr_ref, mask_ref, out_ref,
         qbuf, kv, bias, bias_out, s_ref, o_own, st_own, o_out, st_out, o_in, st_in,
         ld_sem, zs, zr, xs, xr, bs, br, osd, orv, sts, str_) = refs
    frame = lax.axis_index("frame")
    row = lax.axis_index("row")
    me = frame * n_row + row
    coef = jnp.float32(SCALE * LOG2E)

    def cols(h):
        return pl.ds(pl.multiple_of(h * HEAD_DIM, HEAD_DIM), HEAD_DIM)

    def load(h):
        return (
            pltpu.make_async_copy(k_hbm.at[:, cols(h)], kv.at[0, h, 0], ld_sem.at[0, h]),
            pltpu.make_async_copy(v_hbm.at[:, cols(h)], kv.at[0, h, 1], ld_sem.at[1, h]),
            pltpu.make_async_copy(q_hbm.at[:, cols(h)], qbuf.at[0, h], ld_sem.at[2, h]),
        )

    for h in range(heads):
        for copy in load(h):
            copy.start()

    frame_links = (
        (1, {"frame": frame + 1}, frame < n_frame - 1, 0),
        (2, {"frame": frame - 1}, frame > 0, 1),
    )
    if nbrs == 0:
        row_links = ()
    elif nbrs == 1:
        row_links = ((0, {"row": 1 - row}, None),)
    else:
        row_links = ((1, {"row": row - 1}, row > 0), (0, {"row": row + 1}, row < n_row - 1))

    def guarded(cond, fn):
        if cond is None:
            fn()
        else:
            pl.when(cond)(fn)

    barrier = pltpu.get_barrier_semaphore()
    if with_regs:
        for k in range(1, peers):
            peer = lax.rem(me + k, peers)
            pl.semaphore_signal(
                barrier, inc=1, device_id={"frame": peer // n_row, "row": lax.rem(peer, n_row)},
                device_id_type=MESH,
            )
        pl.semaphore_wait(barrier, peers - 1)
    else:
        links = [(dev, ok) for _, dev, ok, _ in frame_links] + [(dev, ok) for _, dev, ok in row_links]
        for dev, ok in links:
            guarded(ok, lambda dev=dev: pl.semaphore_signal(
                barrier, inc=1, device_id=dev, device_id_type=MESH))
        for dev, ok in links:
            guarded(ok, lambda: pl.semaphore_wait(barrier, 1))

    def kv_copy(h, link):
        slot, dev, _, i = link
        return pltpu.make_async_remote_copy(
            src_ref=kv.at[0, h], dst_ref=kv.at[slot, h], send_sem=zs.at[i, h],
            recv_sem=zr.at[slot - 1, h], device_id=dev, device_id_type=MESH)

    def q_copy(h, j):
        theirs, dev, _ = row_links[j]
        return pltpu.make_async_remote_copy(
            src_ref=qbuf.at[0, h], dst_ref=qbuf.at[1 + theirs, h], send_sem=xs.at[j, h],
            recv_sem=xr.at[theirs, h], device_id=dev, device_id_type=MESH)

    def bias_copy(j):
        theirs, dev, _ = row_links[j]
        return pltpu.make_async_remote_copy(
            src_ref=bias_out.at[j], dst_ref=bias.at[1 + theirs], send_sem=bs.at[j],
            recv_sem=br.at[theirs], device_id=dev, device_id_type=MESH)

    def o_copy(h, j):
        theirs, dev, _ = row_links[j]
        return (
            pltpu.make_async_remote_copy(
                src_ref=o_out.at[j, h], dst_ref=o_in.at[theirs, h], send_sem=osd.at[j, h],
                recv_sem=orv.at[theirs, h], device_id=dev, device_id_type=MESH),
            pltpu.make_async_remote_copy(
                src_ref=st_out.at[j, h], dst_ref=st_in.at[theirs, h], send_sem=sts.at[j, h],
                recv_sem=str_.at[theirs, h], device_id=dev, device_id_type=MESH),
        )

    for h in range(heads):
        copies = load(h)
        copies[0].wait()
        copies[1].wait()
        for link in frame_links:
            guarded(link[2], lambda link=link: kv_copy(h, link).start())
        copies[2].wait()
        for j in range(nbrs):
            guarded(row_links[j][2], lambda j=j: q_copy(h, j).start())

    lane_tile = (lax.broadcasted_iota(jnp.int32, (1, tokens), 1) % columns) // tile_c
    frame_ok = [None, (frame > 0).astype(jnp.int32), (frame < n_frame - 1).astype(jnp.int32)]
    bias[0] = jnp.zeros(bias.shape[1:], bias.dtype)
    if nbrs:
        bias_out[...] = jnp.zeros_like(bias_out)
    for target in range(1 + nbrs):
        for slot, df in enumerate(SLOT_DF):
            for tk in range(col_tiles):
                vec = jnp.full((1, tokens), NEG, jnp.float32)
                for tq in range(col_tiles):
                    dc = tk - tq
                    if abs(dc) > 1:
                        continue
                    if target == 0:
                        if df == 0 and dc == 0:
                            ok = jnp.int32(1)
                        else:
                            ok = mask_ref[0, 0, tq, offset_index(df, 0, dc)]
                    elif nbrs == 1:
                        plus, minus = offset_index(df, 1, dc), offset_index(df, -1, dc)
                        ok = mask_ref[0, 0, tq, plus + row * (minus - plus)]
                    else:
                        ok = mask_ref[0, 0, tq, offset_index(df, (-1, 1)[target - 1], dc)]
                    if frame_ok[slot] is not None:
                        ok = ok * frame_ok[slot]
                    vec = jnp.where(lane_tile == tq, (ok.astype(jnp.float32) - 1.0) * -NEG, vec)
                r = slot * col_tiles + tk
                if target == 0:
                    bias[0, r:r + 1, :] = vec
                else:
                    bias_out[target - 1, r:r + 1, :] = vec
    for j in range(nbrs):
        guarded(row_links[j][2], lambda j=j: bias_copy(j).start())

    @pl.when(frame == 0)
    def _():
        kv[1] = jnp.zeros(kv.shape[1:], kv.dtype)

    @pl.when(frame == n_frame - 1)
    def _():
        kv[2] = jnp.zeros(kv.shape[1:], kv.dtype)

    for j in range(nbrs):
        if row_links[j][2] is not None:
            @pl.when(jnp.logical_not(row_links[j][2]))
            def _():
                qbuf[1 + j] = jnp.zeros(qbuf.shape[1:], qbuf.dtype)
                bias[1 + j] = jnp.zeros(bias.shape[1:], bias.dtype)

    if with_regs:
        own_lane = lax.broadcasted_iota(jnp.int32, (1, regs), 1) // share == me
        reg_bias = jnp.where(own_lane, 0.0, NEG).astype(jnp.float32)

        def reg_head(h, carry):
            qh = qr_ref[:, cols(h)]
            s0 = nt(kv[0, h, 0], qh) * coef
            s1 = nt(kr_ref[:, cols(h)], qh) * coef + reg_bias
            m = jnp.maximum(jnp.max(s0, 0, keepdims=True), jnp.max(s1, 0, keepdims=True))
            p0 = jnp.exp2(s0 - m)
            p1 = jnp.exp2(s1 - m)
            l = jnp.sum(p0, 0, keepdims=True) + jnp.sum(p1, 0, keepdims=True)
            acc = tn(kv[0, h, 1], p0.astype(jnp.bfloat16)) + tn(vr_ref[:, cols(h)], p1.astype(jnp.bfloat16))
            r_out[:, h] = acc.T.reshape(peers, share, HEAD_DIM).astype(jnp.bfloat16)
            rst_t[pl.ds(h, 1), :] = m
            rst_t[pl.ds(heads + h, 1), :] = l
            return carry

        rst_t[...] = jnp.zeros_like(rst_t)
        lax.fori_loop(0, heads, reg_head, 0)
        rst_out[...] = rst_t[...].T.reshape(rst_out.shape)

        def reg_copy(k):
            peer = lax.rem(me + k, peers)
            dev = {"frame": peer // n_row, "row": lax.rem(peer, n_row)}
            return (
                pltpu.make_async_remote_copy(
                    src_ref=r_out.at[peer], dst_ref=r_in.at[k], send_sem=rs.at[0, k],
                    recv_sem=rr.at[0, k], device_id=dev, device_id_type=MESH),
                pltpu.make_async_remote_copy(
                    src_ref=rst_out.at[peer], dst_ref=rst_in.at[k], send_sem=rs.at[1, k],
                    recv_sem=rr.at[1, k], device_id=dev, device_id_type=MESH),
            )

        for k in range(1, peers):
            for copy in reg_copy(k):
                copy.start()

    for j in range(nbrs):
        guarded(row_links[j][2], lambda j=j: pltpu.make_async_remote_copy(
            src_ref=bias_out.at[j], dst_ref=bias.at[1 + j], send_sem=bs.at[j], recv_sem=br.at[j],
            device_id=row_links[j][1], device_id_type=MESH).wait_recv())

    lanes = (1 + nbrs) * tokens

    def video_head(h, carry):
        for j in range(nbrs):
            guarded(row_links[j][2], lambda j=j: pltpu.make_async_remote_copy(
                src_ref=qbuf.at[0, h], dst_ref=qbuf.at[1 + j, h], send_sem=xs.at[j, h],
                recv_sem=xr.at[j, h], device_id=row_links[j][1], device_id_type=MESH).wait_recv())
        qall = qbuf[:, h].reshape(lanes, HEAD_DIM)
        m = None
        for slot in range(3):
            if slot:
                there = (frame > 0) if slot == 1 else (frame < n_frame - 1)
                dev = {"frame": frame - 1} if slot == 1 else {"frame": frame + 1}
                guarded(there, lambda: pltpu.make_async_remote_copy(
                    src_ref=kv.at[0, h], dst_ref=kv.at[slot, h], send_sem=zs.at[slot - 1, h],
                    recv_sem=zr.at[slot - 1, h], device_id=dev, device_id_type=MESH).wait_recv())
            s = nt(kv[slot, h, 0], qall) * coef
            rows = bias[:, slot * col_tiles:(slot + 1) * col_tiles, :]
            rows = jnp.concatenate([rows[t] for t in range(1 + nbrs)], axis=1)
            s = s.reshape(tokens // columns, col_tiles, tile_c, lanes) + rows[None, :, None, :]
            s = s.reshape(tokens, lanes)
            s_ref[slot * tokens:(slot + 1) * tokens, :] = s
            top = jnp.max(s, 0, keepdims=True)
            m = top if m is None else jnp.maximum(m, top)
        sr = nt(kr_ref[:, cols(h)], qall[:tokens]) * coef
        m_own = jnp.maximum(m[:, :tokens], jnp.max(sr, 0, keepdims=True))
        m = jnp.concatenate([m_own, m[:, tokens:]], axis=1) if nbrs else m_own
        pr = jnp.exp2(sr - m_own)
        l = None
        o = None
        for slot in range(3):
            p = jnp.exp2(s_ref[slot * tokens:(slot + 1) * tokens, :] - m)
            total = jnp.sum(p, 0, keepdims=True)
            part = tn(kv[slot, h, 1], p.astype(jnp.bfloat16))
            l = total if l is None else l + total
            o = part if o is None else o + part
        for j in range(nbrs):
            sl = slice((1 + j) * tokens, (2 + j) * tokens)
            o_out[j, h] = o[:, sl].astype(jnp.bfloat16)
            st_out[j, h] = jnp.concatenate([m[:, sl]] * 4 + [l[:, sl]] * 4, axis=0)

            def send(j=j):
                for copy in o_copy(h, j):
                    copy.start()

            guarded(row_links[j][2], send)
        o_own[h] = o[:, :tokens] + tn(vr_ref[:, cols(h)], pr.astype(jnp.bfloat16))
        l_own = l[:, :tokens] + jnp.sum(pr, 0, keepdims=True)
        st_own[h] = jnp.concatenate([m_own] * 4 + [l_own] * 4, axis=0)
        return carry

    for j in range(nbrs):
        if row_links[j][2] is not None:
            @pl.when(jnp.logical_not(row_links[j][2]))
            def _():
                o_in[j] = jnp.zeros(o_in.shape[1:], o_in.dtype)
                st_in[j] = jnp.full(st_in.shape[1:], NEG, st_in.dtype)

    lax.fori_loop(0, heads, video_head, 0)

    def finish_head(h, carry):
        st = st_own[h]
        m, l, o = st[0:1], st[4:5], o_own[h]
        parts = []
        for j in range(nbrs):
            def arrive(j=j):
                pltpu.make_async_remote_copy(
                    src_ref=o_out.at[j, h], dst_ref=o_in.at[j, h], send_sem=osd.at[j, h],
                    recv_sem=orv.at[j, h], device_id=row_links[j][1], device_id_type=MESH).wait_recv()
                pltpu.make_async_remote_copy(
                    src_ref=st_out.at[j, h], dst_ref=st_in.at[j, h], send_sem=sts.at[j, h],
                    recv_sem=str_.at[j, h], device_id=row_links[j][1], device_id_type=MESH).wait_recv()

            guarded(row_links[j][2], arrive)
            other = st_in[j, h]
            parts.append((other[0:1], other[4:5], o_in[j, h].astype(jnp.float32)))
        joint = m
        for mj, _, _ in parts:
            joint = jnp.maximum(joint, mj)
        factor = jnp.exp2(m - joint)
        total = l * factor
        factors = []
        for mj, lj, _ in parts:
            fj = jnp.exp2(mj - joint)
            factors.append(fj)
            total = total + lj * fj
        inv = 1.0 / total
        o = o * (factor * inv)
        for fj, (_, _, oj) in zip(factors, parts):
            o = o + oj * (fj * inv)
        out_ref[:, cols(h)] = o.T.astype(jnp.bfloat16)
        return carry

    lax.fori_loop(0, heads, finish_head, 0)

    if with_regs:
        for k in range(1, peers):
            for copy in reg_copy(k):
                copy.wait_recv()
        for h in range(heads):
            ms = [rst_out[me][:, h:h + 1]] + [rst_in[k][:, h:h + 1] for k in range(1, peers)]
            ls = [rst_out[me][:, heads + h:heads + h + 1]] + [
                rst_in[k][:, heads + h:heads + h + 1] for k in range(1, peers)]
            accs = [r_out[me, h]] + [r_in[k, h] for k in range(1, peers)]
            joint = functools.reduce(jnp.maximum, ms)
            total = None
            acc = None
            for mk, lk, ak in zip(ms, ls, accs):
                f = jnp.exp2(mk - joint)
                tk, wk = lk * f, ak.astype(jnp.float32) * f
                total = tk if total is None else total + tk
                acc = wk if acc is None else acc + wk
            outr_ref[:, h * HEAD_DIM:(h + 1) * HEAD_DIM] = (acc / total).astype(jnp.bfloat16)

    def sent(h, carry):
        for link in frame_links:
            guarded(link[2], lambda link=link: kv_copy(h, link).wait_send())
        for j in range(nbrs):
            def left(j=j):
                q_copy(h, j).wait_send()
                for copy in o_copy(h, j):
                    copy.wait_send()

            guarded(row_links[j][2], left)
        return carry

    lax.fori_loop(0, heads, sent, 0)
    for j in range(nbrs):
        guarded(row_links[j][2], lambda j=j: bias_copy(j).wait_send())
    if with_regs:
        for k in range(1, peers):
            for copy in reg_copy(k):
                copy.wait_send()


def exact_product(weights, values):
    leading = weights.astype(values.dtype)
    remainder = (weights - leading.astype(weights.dtype)).astype(values.dtype)
    return jnp.einsum("hqk,khd->hqd", leading, values, preferred_element_type=jnp.float32) + jnp.einsum(
        "hqk,khd->hqd", remainder, values, preferred_element_type=jnp.float32)


def partial_softmax(queries, keys, values):
    scores = jnp.einsum("qhd,khd->hqk", queries, keys, preferred_element_type=jnp.float32) * SCALE
    top = jnp.max(scores, axis=-1)
    weights = jnp.exp(scores - top[..., None])
    return top, jnp.sum(weights, axis=-1), exact_product(weights, values)


def registers_by_reduction(q_reg, k_reg, v_reg, k_video, v_video, heads, share):
    split = lambda x: x.reshape(-1, heads, HEAD_DIM)
    start = (lax.axis_index("frame") * lax.axis_size("row") + lax.axis_index("row")) * share
    top, total, weighted = partial_softmax(split(q_reg), split(k_video), split(v_video))
    joint = lax.pmax(top, ("frame", "row"))
    factor = jnp.exp(top - joint)
    total, weighted = lax.psum((total * factor, weighted * factor[..., None]), ("frame", "row"))
    own = lambda x: lax.dynamic_slice_in_dim(x, start, share, 1)
    queries = lax.dynamic_slice_in_dim(q_reg, start, share, 0)
    top2, total2, weighted2 = partial_softmax(split(queries), split(k_reg), split(v_reg))
    top1, total1, weighted1 = own(joint), own(total), own(weighted)
    last = jnp.maximum(top1, top2)
    f1, f2 = jnp.exp(top1 - last), jnp.exp(top2 - last)
    out = (weighted1 * f1[..., None] + weighted2 * f2[..., None]) / (total1 * f1 + total2 * f2)[..., None]
    return out.transpose(1, 0, 2).reshape(share, heads * HEAD_DIM).astype(jnp.bfloat16)


def on_device(q_video, k_video, v_video, q_reg, k_reg, v_reg, nbr_mask):
    tile_f, tile_r, columns, features = q_video.shape
    col_tiles = nbr_mask.shape[2]
    tile_c = columns // col_tiles
    tokens = tile_f * tile_r * columns
    heads = features // HEAD_DIM
    regs = q_reg.shape[0]
    n_frame, n_row = lax.axis_size("frame"), lax.axis_size("row")
    peers = n_frame * n_row
    share = regs // peers
    with_regs = share % 8 == 0 and 2 * heads <= 128
    nbrs = 0 if n_row == 1 else (1 if n_row == 2 else 2)
    nslot = max(nbrs, 1)
    bias_rows = -(-3 * col_tiles // 8) * 8
    dims = (heads, tokens, columns, tile_c, col_tiles, regs, n_frame, n_row, with_regs)
    bf16, f32 = jnp.bfloat16, jnp.float32
    dma = lambda *shape: pltpu.SemaphoreType.DMA(shape)
    scratch = [
        pltpu.VMEM((1 + nbrs, heads, tokens, HEAD_DIM), bf16),
        pltpu.VMEM((3, heads, 2, tokens, HEAD_DIM), bf16),
        pltpu.VMEM((1 + nbrs, bias_rows, tokens), f32),
        pltpu.VMEM((nslot, bias_rows, tokens), f32),
        pltpu.VMEM((3 * tokens, (1 + nbrs) * tokens), f32),
        pltpu.VMEM((heads, HEAD_DIM, tokens), f32),
        pltpu.VMEM((heads, 8, tokens), f32),
        pltpu.VMEM((nslot, heads, HEAD_DIM, tokens), bf16),
        pltpu.VMEM((nslot, heads, 8, tokens), f32),
        pltpu.VMEM((nslot, heads, HEAD_DIM, tokens), bf16),
        pltpu.VMEM((nslot, heads, 8, tokens), f32),
        dma(3, heads), dma(2, heads), dma(2, heads), dma(nslot, heads), dma(nslot, heads),
        dma(nslot), dma(nslot), dma(nslot, heads), dma(nslot, heads), dma(nslot, heads), dma(nslot, heads),
    ]
    out_shape = [jax.ShapeDtypeStruct((tokens, features), bf16)]
    any_spec, vmem, smem = (pl.BlockSpec(memory_space=s) for s in (pl.ANY, pltpu.VMEM, pltpu.SMEM))
    if with_regs:
        scratch += [
            pltpu.VMEM((peers, heads, share, HEAD_DIM), bf16),
            pltpu.VMEM((128, regs), f32),
            pltpu.VMEM((peers, share, 128), f32),
            pltpu.VMEM((peers, heads, share, HEAD_DIM), bf16),
            pltpu.VMEM((peers, share, 128), f32),
            dma(2, peers), dma(2, peers),
        ]
        out_shape.append(jax.ShapeDtypeStruct((share, features), bf16))
        reg_args = (q_reg, k_reg, v_reg)
    else:
        reg_args = (k_reg, v_reg)
    flat = lambda x: x.reshape(tokens, features)
    outs = pl.pallas_call(
        functools.partial(block_kernel, dims),
        out_shape=out_shape,
        in_specs=[any_spec] * 3 + [vmem] * len(reg_args) + [smem],
        out_specs=[vmem] * len(out_shape),
        scratch_shapes=scratch,
        compiler_params=pltpu.CompilerParams(
            collective_id=0, has_side_effects=True, vmem_limit_bytes=40 * 1024 * 1024),
    )(flat(q_video), flat(k_video), flat(v_video), *reg_args, nbr_mask)
    out_video = outs[0].reshape(q_video.shape)
    if with_regs:
        out_reg = outs[1]
    else:
        out_reg = registers_by_reduction(q_reg, k_reg, v_reg, k_video, v_video, heads, share)
    return out_video, out_reg


def solution(mesh):
    video = P(("group", "frame"), "row", None, "head")
    reg = P("group", "head")
    return jax.shard_map(
        on_device,
        mesh=mesh,
        in_specs=(video, video, video, reg, reg, reg, P("frame", "row", None, None)),
        out_specs=(video, P(("group", "frame", "row"), "head")),
        check_vma=False,
    )
```

time: 392 us -> 41.5 us (0.11); the launches traced: 386 us -> 41.2 us
  other arithmetic: 164 us -> 0 us
  blocking collectives: 66.4 us -> 0 us
  local copies, waits for them, and re-layouts: 58.4 us -> 7.79 us
  matrix products: 38.3 us -> 0 us
  loops' own time: 33.3 us -> 0 us
  Pallas kernels: 0 us -> 32.7 us
  between operations: 14.2 us -> 0.66 us
  starting transfers between devices: 10.4 us -> 0 us
    select_n x12 -> x0, other arithmetic: 84.1 us -> none  [one_item(): jnp.repeat(allowed.reshape(-1), tile_size, total_repeat_length=9 * window...]
    gather x12 -> x0, other arithmetic: 56.4 us -> none  [one_item(): jnp.repeat(allowed.reshape(-1), tile_size, total_repeat_length=9 * window...]
    psum x1 -> x0, blocking collectives: 43.7 us -> none  [on_device(): lax.psum((rescale(local_weighted, factor), local_total * factor), ('frame...]
    dot_general x60 -> x0, matrix products: 38.3 us -> none  [the longest x12 12.8 us: partial_softmax(): jnp.dot(query_head, key_head.T, preferred_element_type=jnp.float32)]
    another operation x3 -> x0, loops' own time: 33.3 us -> none  [the longest x1 25 us: on_device(): lax.map(one_item, jnp.arange(col_tiles * heads_dev, dtype=jnp.int32))]
    pallas_call x0 -> x1, Pallas kernels: none -> 32.7 us  [on_device(): pl.pallas_call(functools.partial(block_kernel, dims), out_shape=out_shape...]
    dynamic_slice x37 -> x0, local copies, waits for them, and re-layouts: 24.1 us -> none  [the longest x12 9.27 us: one_item(): lax.dynamic_slice_in_dim(v_reg, head_index * HEAD_DIM, HEAD_DIM, 1)]
    pmax x1 -> x0, blocking collectives: 22.7 us -> none  [on_device(): global_max = lax.pmax(local_max, ('frame', 'row'))]
  transfers between devices with their start and end apart: 5 -> 0, of which waited for: 1 -> 0; matrix products, arithmetic and copies ran while one was open for 11% -> 0% of each run, Pallas kernels for 0% -> 0%
where the time goes in v1:
time: 41.5 us; the launch traced here: 41.2 us
  Pallas kernels  32.7 us (79%)
  local copies, waits for them, and re-layouts  7.79 us (19%)
  between operations  0.66 us (2%)
    pallas_call x1, Pallas kernels, on_device(): pl.pallas_call(functools.partial(block_kernel, dims), out_shape=out_shape...  32.7 us
    unnamed x16, local copies, waits for them, and re-layouts  7.79 us

profile of v1, /device:TPU:0, one launch (start us, length us, event | category | flops | bytes accessed | tf_op | source)
XLA Modules:
  0.0 41.2 jit_solution(3739130118038057619)
XLA Ops:
  0.6 0.0 copy-start.6
  0.6 0.7 %copy-done.6 = s32[1,1,2,26]{3,2,1,0:T(2,128)S(1)} copy-done((s32[1,1,2,26]{3,2,1,0:T(2,128)S(1)}, s32[1,1,2,26]{3,2,1,0:T(2,128)}, u32[]{:S(2)}) %copy-start.6) | copy-done | bytes 232
  1.3 0.0 copy-start
  1.3 1.0 %copy-done = bf16[2,8,16,768]{3,2,1,0:T(8,128)(2,1)S(1)} copy-done((bf16[2,8,16,768]{3,2,1,0:T(8,128)(2,1)S(1)}, bf16[2,8,16,768]{3,2,1,0:T(8,128)(2,1)}, u32[]{:S(2)}) %copy-start) | copy-done | bytes 393240
  2.3 0.0 copy-start.1
  2.3 1.0 %copy-done.1 = bf16[2,8,16,768]{3,2,1,0:T(8,128)(2,1)S(1)} copy-done((bf16[2,8,16,768]{3,2,1,0:T(8,128)(2,1)S(1)}, bf16[2,8,16,768]{3,2,1,0:T(8,128)(2,1)}, u32[]{:S(2)}) %copy-start.1) | copy-done | bytes 393240
  3.3 0.0 copy-start.2
  3.3 1.0 %copy-done.2 = bf16[2,8,16,768]{3,2,1,0:T(8,128)(2,1)S(1)} copy-done((bf16[2,8,16,768]{3,2,1,0:T(8,128)(2,1)S(1)}, bf16[2,8,16,768]{3,2,1,0:T(8,128)(2,1)}, u32[]{:S(2)}) %copy-start.2) | copy-done | bytes 393240
  4.3 0.0 copy-start.3
  4.3 0.9 %copy-done.3 = bf16[128,768]{1,0:T(8,128)(2,1)S(1)} copy-done((bf16[128,768]{1,0:T(8,128)(2,1)S(1)}, bf16[128,768]{1,0:T(8,128)(2,1)}, u32[]{:S(2)}) %copy-start.3) | copy-done | bytes 196632
  5.2 0.0 copy-start.4
  5.2 0.9 %copy-done.4 = bf16[128,768]{1,0:T(8,128)(2,1)S(1)} copy-done((bf16[128,768]{1,0:T(8,128)(2,1)S(1)}, bf16[128,768]{1,0:T(8,128)(2,1)}, u32[]{:S(2)}) %copy-start.4) | copy-done | bytes 196632
  6.2 0.0 copy-start.5
  6.2 0.9 %copy-done.5 = bf16[128,768]{1,0:T(8,128)(2,1)S(1)} copy-done((bf16[128,768]{1,0:T(8,128)(2,1)S(1)}, bf16[128,768]{1,0:T(8,128)(2,1)}, u32[]{:S(2)}) %copy-start.5) | copy-done | bytes 196632
  7.1 32.7 %shard_map.86 = (bf16[256,768]{1,0:T(8,128)(2,1)S(1)}, bf16[16,768]{1,0:T(8,128)(2,1)S(1)}) custom-call(bf16[256,768]{1,0:T(8,128)(2,1)S(1)} %bitcast.5, bf16[256,768]{1,0:T(8,128)(2,1)S(1)} %bitcast.6, bf16[256,768]{1,0:T(8,128)(2,1)S(1)} %bitcast.7, bf16[128,768]{1,0:T(8,128)(2,1)S(1)} %copy-done.3, bf16[128,768]{1,0:T(8,128)(2,1)S(1)} %copy-done.4, ...), custom_call_target="tpu_custom_call" | custom-call | tf_op jit(solution)/shard_map/pallas_call | solution.py:443
  39.8 0.7 %copy.11 = bf16[2,8,16,768]{3,2,1,0:T(8,128)(2,1)} copy(bf16[2,8,16,768]{3,2,1,0:T(8,128)(2,1)S(1)} %bitcast.4) | data formatting | bytes 786432
  40.6 0.6 %copy.12 = bf16[16,768]{1,0:T(8,128)(2,1)} copy(bf16[16,768]{1,0:T(8,128)(2,1)S(1)} %get-tuple-element.9) | data formatting | bytes 49152
Async XLA Ops:
  0.6 0.7 %copy-start.6 = (s32[1,1,2,26]{3,2,1,0:T(2,128)S(1)}, s32[1,1,2,26]{3,2,1,0:T(2,128)}, u32[]{:S(2)}) copy-start(s32[1,1,2,26]{3,2,1,0:T(2,128)} %refs_6_.1) | copy-start | bytes 628
  1.3 1.0 %copy-start = (bf16[2,8,16,768]{3,2,1,0:T(8,128)(2,1)S(1)}, bf16[2,8,16,768]{3,2,1,0:T(8,128)(2,1)}, u32[]{:S(2)}) copy-start(bf16[2,8,16,768]{3,2,1,0:T(8,128)(2,1)} %param.7) | copy-start | bytes 1179652
  2.3 1.0 %copy-start.1 = (bf16[2,8,16,768]{3,2,1,0:T(8,128)(2,1)S(1)}, bf16[2,8,16,768]{3,2,1,0:T(8,128)(2,1)}, u32[]{:S(2)}) copy-start(bf16[2,8,16,768]{3,2,1,0:T(8,128)(2,1)} %param.8) | copy-start | bytes 1179652
  3.3 1.0 %copy-start.2 = (bf16[2,8,16,768]{3,2,1,0:T(8,128)(2,1)S(1)}, bf16[2,8,16,768]{3,2,1,0:T(8,128)(2,1)}, u32[]{:S(2)}) copy-start(bf16[2,8,16,768]{3,2,1,0:T(8,128)(2,1)} %param.9) | copy-start | bytes 1179652
  4.3 0.9 %copy-start.3 = (bf16[128,768]{1,0:T(8,128)(2,1)S(1)}, bf16[128,768]{1,0:T(8,128)(2,1)}, u32[]{:S(2)}) copy-start(bf16[128,768]{1,0:T(8,128)(2,1)} %refs_3_.1) | copy-start | bytes 589828
  5.2 0.9 %copy-start.4 = (bf16[128,768]{1,0:T(8,128)(2,1)S(1)}, bf16[128,768]{1,0:T(8,128)(2,1)}, u32[]{:S(2)}) copy-start(bf16[128,768]{1,0:T(8,128)(2,1)} %refs_4_.1) | copy-start | bytes 589828
  6.2 0.9 %copy-start.5 = (bf16[128,768]{1,0:T(8,128)(2,1)S(1)}, bf16[128,768]{1,0:T(8,128)(2,1)}, u32[]{:S(2)}) copy-start(bf16[128,768]{1,0:T(8,128)(2,1)} %refs_5_.1) | copy-start | bytes 589828

commit v2 on v1

--- a/solution.py
+++ b/solution.py
@@ -34,13 +34,13 @@
     share = regs // peers
     nbrs = 0 if n_row == 1 else (1 if n_row == 2 else 2)
     if with_regs:
-        (q_hbm, k_hbm, v_hbm, qr_ref, kr_ref, vr_ref, mask_ref, out_ref, outr_ref,
-         qbuf, kv, bias, bias_out, s_ref, o_own, st_own, o_out, st_out, o_in, st_in,
+        (q_hbm, k_hbm, v_hbm, qr_hbm, kr_hbm, vr_hbm, mask_hbm, out_ref, outr_ref,
+         kr_ref, vr_ref, mask_ref, ld_reg, qbuf, kv, bias, bias_out, s_ref, o_own, st_own, o_out, st_out, o_in, st_in,
          ld_sem, zs, zr, xs, xr, bs, br, osd, orv, sts, str_,
-         r_out, rst_t, rst_out, r_in, rst_in, rs, rr) = refs
+         qr_ref, r_out, rst_t, rst_out, r_in, rst_in, rs, rr) = refs
     else:
-        (q_hbm, k_hbm, v_hbm, kr_ref, vr_ref, mask_ref, out_ref,
-         qbuf, kv, bias, bias_out, s_ref, o_own, st_own, o_out, st_out, o_in, st_in,
+        (q_hbm, k_hbm, v_hbm, kr_hbm, vr_hbm, mask_hbm, out_ref,
+         kr_ref, vr_ref, mask_ref, ld_reg, qbuf, kv, bias, bias_out, s_ref, o_own, st_own, o_out, st_out, o_in, st_in,
          ld_sem, zs, zr, xs, xr, bs, br, osd, orv, sts, str_) = refs
     frame = lax.axis_index("frame")
     row = lax.axis_index("row")
@@ -60,6 +60,13 @@
     for h in range(heads):
         for copy in load(h):
             copy.start()
+        if h == 0:
+            small = [(mask_hbm, mask_ref), (kr_hbm, kr_ref), (vr_hbm, vr_ref)]
+            if with_regs:
+                small.append((qr_hbm, qr_ref))
+            small = [pltpu.make_async_copy(a, b, ld_reg.at[i]) for i, (a, b) in enumerate(small)]
+            for copy in small:
+                copy.start()
 
     frame_links = (
         (1, {"frame": frame + 1}, frame < n_frame - 1, 0),
@@ -133,6 +140,9 @@
         copies[2].wait()
         for j in range(nbrs):
             guarded(row_links[j][2], lambda j=j: q_copy(h, j).start())
+
+    for copy in small:
+        copy.wait()
 
     lane_tile = (lax.broadcasted_iota(jnp.int32, (1, tokens), 1) % columns) // tile_c
     frame_ok = [None, (frame > 0).astype(jnp.int32), (frame < n_frame - 1).astype(jnp.int32)]
@@ -319,8 +329,6 @@
         out_ref[:, cols(h)] = o.T.astype(jnp.bfloat16)
         return carry
 
-    lax.fori_loop(0, heads, finish_head, 0)
-
     if with_regs:
         for k in range(1, peers):
             for copy in reg_copy(k):
@@ -339,6 +347,8 @@
                 total = tk if total is None else total + tk
                 acc = wk if acc is None else acc + wk
             outr_ref[:, h * HEAD_DIM:(h + 1) * HEAD_DIM] = (acc / total).astype(jnp.bfloat16)
+
+    lax.fori_loop(0, heads, finish_head, 0)
 
     def sent(h, carry):
         for link in frame_links:
@@ -410,6 +420,8 @@
     bf16, f32 = jnp.bfloat16, jnp.float32
     dma = lambda *shape: pltpu.SemaphoreType.DMA(shape)
     scratch = [
+        pltpu.VMEM((regs, features), bf16), pltpu.VMEM((regs, features), bf16),
+        pltpu.SMEM(nbr_mask.shape, jnp.int32), dma(4),
         pltpu.VMEM((1 + nbrs, heads, tokens, HEAD_DIM), bf16),
         pltpu.VMEM((3, heads, 2, tokens, HEAD_DIM), bf16),
         pltpu.VMEM((1 + nbrs, bias_rows, tokens), f32),
@@ -425,9 +437,10 @@
         dma(nslot), dma(nslot), dma(nslot, heads), dma(nslot, heads), dma(nslot, heads), dma(nslot, heads),
     ]
     out_shape = [jax.ShapeDtypeStruct((tokens, features), bf16)]
-    any_spec, vmem, smem = (pl.BlockSpec(memory_space=s) for s in (pl.ANY, pltpu.VMEM, pltpu.SMEM))
+    hbm, vmem = (pl.BlockSpec(memory_space=s) for s in (pltpu.HBM, pltpu.VMEM))
     if with_regs:
         scratch += [
+            pltpu.VMEM((regs, features), bf16),
             pltpu.VMEM((peers, heads, share, HEAD_DIM), bf16),
             pltpu.VMEM((128, regs), f32),
             pltpu.VMEM((peers, share, 128), f32),
@@ -443,11 +456,11 @@
     outs = pl.pallas_call(
         functools.partial(block_kernel, dims),
         out_shape=out_shape,
-        in_specs=[any_spec] * 3 + [vmem] * len(reg_args) + [smem],
+        in_specs=[hbm] * (4 + len(reg_args)),
         out_specs=[vmem] * len(out_shape),
         scratch_shapes=scratch,
         compiler_params=pltpu.CompilerParams(
-            collective_id=0, has_side_effects=True, vmem_limit_bytes=40 * 1024 * 1024),
+            collective_id=0, has_side_effects=True, vmem_limit_bytes=63 * 1024 * 1024),
     )(flat(q_video), flat(k_video), flat(v_video), *reg_args, nbr_mask)
     out_video = outs[0].reshape(q_video.shape)
     if with_regs:

time: 41.5 us -> 35.4 us (0.85)
  local copies, waits for them, and re-layouts: 7.79 us -> 2.38 us
  Pallas kernels: 32.7 us -> 32.2 us
    unnamed x16 -> x4, local copies, waits for them, and re-layouts: 7.79 us -> 2.38 us
    pallas_call x1, Pallas kernels: 32.7 us -> 32.2 us  [on_device(): pl.pallas_call(functools.partial(block_kernel, dims), out_shape=out_shape...]
where the time goes in v2:
time: 35.4 us; the launch traced here: 35.3 us
  Pallas kernels  32.2 us (91%)
  local copies, waits for them, and re-layouts  2.38 us (7%)
  between operations  0.65 us (2%)
    pallas_call x1, Pallas kernels, on_device(): pl.pallas_call(functools.partial(block_kernel, dims), out_shape=out_shape...  32.2 us
    unnamed x4, local copies, waits for them, and re-layouts  2.38 us

profile of v2, /device:TPU:0, one launch (start us, length us, event | category | flops | bytes accessed | tf_op | source)
XLA Modules:
  0.0 35.3 jit_solution(1228062503934775851)
XLA Ops:
  0.6 32.2 %shard_map.86 = (bf16[256,768]{1,0:T(8,128)(2,1)}, bf16[16,768]{1,0:T(8,128)(2,1)}) custom-call(bf16[256,768]{1,0:T(8,128)(2,1)} %bitcast.5, bf16[256,768]{1,0:T(8,128)(2,1)} %bitcast.6, bf16[256,768]{1,0:T(8,128)(2,1)} %bitcast.7, bf16[128,768]{1,0:T(8,128)(2,1)} %refs_3_.1, bf16[128,768]{1,0:T(8,128)(2,1)} %refs_4_.1, bf16[128,768]{1,0:T(8,128)(2,1)} %refs_5_.1, ...), custom_call_target="tpu_custom_call" | custom-call | tf_op jit(solution)/shard_map/pallas_call | solution.py:456
  32.9 0.0 copy-start
  32.9 1.8 %copy.11 = bf16[2,8,16,768]{3,2,1,0:T(8,128)(2,1)} copy(bf16[2,8,16,768]{3,2,1,0:T(8,128)(2,1)} %bitcast.4) | data formatting | bytes 786432
  34.7 0.0 copy-done
  34.7 0.6 %copy.12 = bf16[16,768]{1,0:T(8,128)(2,1)} copy(bf16[16,768]{1,0:T(8,128)(2,1)S(1)} %copy-done) | data formatting | bytes 49152
Async XLA Ops:
  32.9 1.8 %copy-start = (bf16[16,768]{1,0:T(8,128)(2,1)S(1)}, bf16[16,768]{1,0:T(8,128)(2,1)}, u32[]{:S(2)}) copy-start(bf16[16,768]{1,0:T(8,128)(2,1)} %get-tuple-element.9) | copy-start | bytes 73732

commit v3 on v2

--- a/solution.py
+++ b/solution.py
@@ -460,8 +460,8 @@
         out_specs=[vmem] * len(out_shape),
         scratch_shapes=scratch,
         compiler_params=pltpu.CompilerParams(
-            collective_id=0, has_side_effects=True, vmem_limit_bytes=63 * 1024 * 1024),
-    )(flat(q_video), flat(k_video), flat(v_video), *reg_args, nbr_mask)
+            collective_id=0, has_side_effects=True, vmem_limit_bytes=40 * 1024 * 1024),
+    )(*(pltpu.with_memory_space_constraint(x, pltpu.HBM) for x in (flat(q_video), flat(k_video), flat(v_video), *reg_args, nbr_mask)))
     out_video = outs[0].reshape(q_video.shape)
     if with_regs:
         out_reg = outs[1]

time: 35.4 us -> 33.6 us (0.949)
  local copies, waits for them, and re-layouts: 2.38 us -> 1.36 us
  Pallas kernels: 32.2 us -> 31.5 us
    unnamed x4 -> x2, local copies, waits for them, and re-layouts: 2.38 us -> 1.36 us
    pallas_call x1, Pallas kernels: 32.2 us -> 31.5 us  [on_device(): pl.pallas_call(functools.partial(block_kernel, dims), out_shape=out_shape...]
where the time goes in v3:
time: 33.6 us; the launch traced here: 33.5 us
  Pallas kernels  31.5 us (94%)
  local copies, waits for them, and re-layouts  1.36 us (4%)
  between operations  0.64 us (2%)
    pallas_call x1, Pallas kernels, on_device(): pl.pallas_call(functools.partial(block_kernel, dims), out_shape=out_shape...  31.5 us
    unnamed x2, local copies, waits for them, and re-layouts  1.36 us

profile of v3, /device:TPU:0, one launch (start us, length us, event | category | flops | bytes accessed | tf_op | source)
XLA Modules:
  0.0 33.5 jit_solution(13856586925295518209)
XLA Ops:
  0.6 31.5 %shard_map.86 = (bf16[256,768]{1,0:T(8,128)(2,1)S(1)}, bf16[16,768]{1,0:T(8,128)(2,1)S(1)}) custom-call(bf16[256,768]{1,0:T(8,128)(2,1)} %bitcast.5, bf16[256,768]{1,0:T(8,128)(2,1)} %bitcast.6, bf16[256,768]{1,0:T(8,128)(2,1)} %bitcast.7, bf16[128,768]{1,0:T(8,128)(2,1)} %refs_3_.1, bf16[128,768]{1,0:T(8,128)(2,1)} %refs_4_.1, bf16[128,768]{1,0:T(8,128)(2,1)} %refs_5_.1, ...), custom_call_target="tpu_custom_call" | custom-call | tf_op jit(solution)/shard_map/pallas_call | solution.py:456
  32.1 0.7 %copy.11 = bf16[2,8,16,768]{3,2,1,0:T(8,128)(2,1)} copy(bf16[2,8,16,768]{3,2,1,0:T(8,128)(2,1)S(1)} %bitcast.4) | data formatting | bytes 786432
  32.9 0.6 %copy.12 = bf16[16,768]{1,0:T(8,128)(2,1)} copy(bf16[16,768]{1,0:T(8,128)(2,1)S(1)} %get-tuple-element.9) | data formatting | bytes 49152

commit v4 on v3

--- a/solution.py
+++ b/solution.py
@@ -37,7 +37,7 @@
         (q_hbm, k_hbm, v_hbm, qr_hbm, kr_hbm, vr_hbm, mask_hbm, out_ref, outr_ref,
          kr_ref, vr_ref, mask_ref, ld_reg, qbuf, kv, bias, bias_out, s_ref, o_own, st_own, o_out, st_out, o_in, st_in,
          ld_sem, zs, zr, xs, xr, bs, br, osd, orv, sts, str_,
-         qr_ref, r_out, rst_t, rst_out, r_in, rst_in, rs, rr) = refs
+         qr_ref, r_out, rst_t, rst_out, r_in, rst_in, rs, rr, relay) = refs
     else:
         (q_hbm, k_hbm, v_hbm, kr_hbm, vr_hbm, mask_hbm, out_ref,
          kr_ref, vr_ref, mask_ref, ld_reg, qbuf, kv, bias, bias_out, s_ref, o_own, st_own, o_out, st_out, o_in, st_in,
@@ -86,21 +86,25 @@
             pl.when(cond)(fn)
 
     barrier = pltpu.get_barrier_semaphore()
-    if with_regs:
-        for k in range(1, peers):
-            peer = lax.rem(me + k, peers)
-            pl.semaphore_signal(
-                barrier, inc=1, device_id={"frame": peer // n_row, "row": lax.rem(peer, n_row)},
-                device_id_type=MESH,
-            )
-        pl.semaphore_wait(barrier, peers - 1)
-    else:
-        links = [(dev, ok) for _, dev, ok, _ in frame_links] + [(dev, ok) for _, dev, ok in row_links]
-        for dev, ok in links:
-            guarded(ok, lambda dev=dev: pl.semaphore_signal(
-                barrier, inc=1, device_id=dev, device_id_type=MESH))
-        for dev, ok in links:
-            guarded(ok, lambda: pl.semaphore_wait(barrier, 1))
+    links = [(dev, ok, slot - 1) for slot, dev, ok, _ in frame_links]
+    links += [(dev, ok, 2 + theirs) for theirs, dev, ok in row_links]
+    inbound = [(frame > 0, 0), (frame < n_frame - 1, 1)] + [(row_links[j][2], 2 + j) for j in range(nbrs)]
+    for dev, ok, _ in links:
+        guarded(ok, lambda dev=dev: pl.semaphore_signal(
+            barrier, inc=1, device_id=dev, device_id_type=MESH))
+    expected = jnp.int32(0)
+    for _, ok, _ in links:
+        expected = expected + (1 if ok is None else ok.astype(jnp.int32))
+    pl.semaphore_wait(barrier, expected)
+
+    def relay_signal(r):
+        for dev, ok, i in links:
+            guarded(ok, lambda dev=dev, i=i: pl.semaphore_signal(
+                relay.at[r, i], inc=1, device_id=dev, device_id_type=MESH))
+
+    def relay_wait(r):
+        for ok, i in inbound:
+            guarded(ok, lambda i=i: pl.semaphore_wait(relay.at[r, i], 1))
 
     def kv_copy(h, link):
         slot, dev, _, i = link
@@ -212,7 +216,15 @@
             return carry
 
         rst_t[...] = jnp.zeros_like(rst_t)
-        lax.fori_loop(0, heads, reg_head, 0)
+        rounds = max(n_frame + n_row - 3, 0)
+        done = 0
+        for r in range(rounds):
+            relay_signal(r)
+            upto = heads * (r + 1) // rounds
+            lax.fori_loop(done, upto, reg_head, 0)
+            done = upto
+            relay_wait(r)
+        lax.fori_loop(done, heads, reg_head, 0)
         rst_out[...] = rst_t[...].T.reshape(rst_out.shape)
 
         def reg_copy(k):
@@ -329,6 +341,8 @@
         out_ref[:, cols(h)] = o.T.astype(jnp.bfloat16)
         return carry
 
+    lax.fori_loop(0, heads - 1, finish_head, 0)
+
     if with_regs:
         for k in range(1, peers):
             for copy in reg_copy(k):
@@ -348,7 +362,7 @@
                 acc = wk if acc is None else acc + wk
             outr_ref[:, h * HEAD_DIM:(h + 1) * HEAD_DIM] = (acc / total).astype(jnp.bfloat16)
 
-    lax.fori_loop(0, heads, finish_head, 0)
+    lax.fori_loop(heads - 1, heads, finish_head, 0)
 
     def sent(h, carry):
         for link in frame_links:
@@ -447,6 +461,7 @@
             pltpu.VMEM((peers, heads, share, HEAD_DIM), bf16),
             pltpu.VMEM((peers, share, 128), f32),
             dma(2, peers), dma(2, peers),
+            pltpu.SemaphoreType.REGULAR((max(n_frame + n_row - 3, 1), 4)),
         ]
         out_shape.append(jax.ShapeDtypeStruct((share, features), bf16))
         reg_args = (q_reg, k_reg, v_reg)

time: 33.6 us -> 32.6 us (0.970)
  Pallas kernels: 31.5 us -> 30.5 us
    pallas_call x1, Pallas kernels: 31.5 us -> 30.5 us  [on_device(): pl.pallas_call(functools.partial(block_kernel, dims), out_shape=out_shape...]
where the time goes in v4:
time: 32.6 us; the launch traced here: 32.5 us
  Pallas kernels  30.5 us (94%)
  local copies, waits for them, and re-layouts  1.36 us (4%)
  between operations  0.64 us (2%)
    pallas_call x1, Pallas kernels, on_device(): pl.pallas_call(functools.partial(block_kernel, dims), out_shape=out_shape...  30.5 us
    unnamed x2, local copies, waits for them, and re-layouts  1.36 us

profile of v4, /device:TPU:0, one launch (start us, length us, event | category | flops | bytes accessed | tf_op | source)
XLA Modules:
  0.0 32.5 jit_solution(2977983222666366991)
XLA Ops:
  0.6 30.5 %shard_map.86 = (bf16[256,768]{1,0:T(8,128)(2,1)S(1)}, bf16[16,768]{1,0:T(8,128)(2,1)S(1)}) custom-call(bf16[256,768]{1,0:T(8,128)(2,1)} %bitcast.5, bf16[256,768]{1,0:T(8,128)(2,1)} %bitcast.6, bf16[256,768]{1,0:T(8,128)(2,1)} %bitcast.7, bf16[128,768]{1,0:T(8,128)(2,1)} %refs_3_.1, bf16[128,768]{1,0:T(8,128)(2,1)} %refs_4_.1, bf16[128,768]{1,0:T(8,128)(2,1)} %refs_5_.1, ...), custom_call_target="tpu_custom_call" | custom-call | tf_op jit(solution)/shard_map/pallas_call | solution.py:471
  31.1 0.7 %copy.11 = bf16[2,8,16,768]{3,2,1,0:T(8,128)(2,1)} copy(bf16[2,8,16,768]{3,2,1,0:T(8,128)(2,1)S(1)} %bitcast.4) | data formatting | bytes 786432
  31.9 0.6 %copy.12 = bf16[16,768]{1,0:T(8,128)(2,1)} copy(bf16[16,768]{1,0:T(8,128)(2,1)S(1)} %get-tuple-element.9) | data formatting | bytes 49152
